TPU v7x, 512 devices: a whole 4x4x16 slice. The times are simulated.
512 devices in a mesh: visit: 64 (over z, y), template: 8 (over x, core).
Axes of the slice: x: 4, y: 4, z: 16, core: 2. Of those that a mesh axis runs over, the one named last changes fastest.
Arguments:
- template: bfloat16 [64, 256, 1152], P('visit', 'template'), may hold values from -5 to 5
- science: bfloat16 [384, 4, 256, 128], P('visit', None, 'template'), may hold values from -27 to 27
- variance: bfloat16 [384, 4, 256, 128], P('visit', None, 'template'), may hold values from 0.5 to 2
- bad_pixels: int32 [384, 4, 256, 128], P('visit', None, 'template'), may hold values 0 or 1
- intersection_patch: int32 [384, 4], P('visit'), may hold values from 0 to 63, as said below
- intersection_block: int32 [384, 4], P('visit'), may hold values from 0 to 7
Outputs:
- significance: float32 [64, 256, 1024], P('visit', 'template')
Inputs may be any that keep to these rules, and one draw needn't show every extreme that they name: `intersection_patch`: each visit's 4 patches are different. Among the 6 visits of one index of visit (an aligned block of rows), every patch that is named is named exactly 2 times, and one patch is named 2 times in every such block.
All inputs are finite; a program needn't handle non-finite values. No bound on the sum of `bad_pixels` on one device may be relied on, other than what follows from the above.
Results may differ from a plain program's by a relative error of at most 0.0032.
Values may be sent and summed in bfloat16 or wider, within the bound.
A program may use at most 128 MiB of HBM per device.

v0:
```python
import jax
import jax.numpy as jnp
from jax import lax
from jax.sharding import PartitionSpec as P

NBLK = 8
MARGIN = 64
HALF = 10
RIDGE = 0.05


def extended(value, sides, width):
    for axis, dim in sides:
        size, length = (lax.axis_size(axis), value.shape[dim])
        up = [(i, (i + 1) % size) for i in range(size - 1)]
        down = [(j, i) for i, j in up]
        last = lax.slice_in_dim(value, length - width, length, axis=dim)
        leading = lax.slice_in_dim(value, 0, width, axis=dim)
        before = lax.ppermute(last, axis, up)
        after = lax.ppermute(leading, axis, down)
        value = jnp.concatenate([before, value, after], axis=dim)
    return value


def basis_taps():
    spread = jnp.arange(2 * HALF + 1, dtype=jnp.float32)
    scaled = (HALF - spread) / 2.5
    hermite = jnp.stack(
        [
            jnp.ones(scaled.shape, jnp.float32),
            2.0 * scaled,
            4.0 * scaled * scaled - 2.0,
            8.0 * scaled * scaled * scaled - 12.0 * scaled,
        ]
    )
    shaped = hermite * jnp.exp(-0.5 * scaled * scaled)
    shaped = shaped / jnp.sqrt(jnp.sum(shaped * shaped, axis=1, keepdims=True))
    return shaped.astype(jnp.bfloat16)


def solve_normal(system):
    unknowns = system.shape[0]
    rows_index = jnp.arange(unknowns)[:, None, None]
    for column in range(unknowns):
        pivot_row = system[column] / system[column, column][None, :]
        factor = system[:, column, :]
        updated = system - factor[:, None, :] * pivot_row[None, :, :]
        system = jnp.where(rows_index == column, pivot_row[None, :, :], updated)
    return system[:, unknowns, :]


def column_table(profile, block_span, block_width):
    offsets = jnp.arange(block_span)[:, None] - jnp.arange(block_width)[None, :] - (MARGIN - HALF)
    choose = (offsets[None] == jnp.arange(2 * HALF + 1)[:, None, None]).astype(jnp.float32)
    toeplitz = jnp.einsum("at,tnc->nac", profile.astype(jnp.float32), choose)
    return toeplitz.reshape(block_span, 4 * block_width).astype(jnp.bfloat16)


def row_table(profile, strip_rows):
    offsets = jnp.arange(strip_rows + 2 * HALF)[None, :] - jnp.arange(strip_rows)[:, None]
    choose = (offsets[None] == jnp.arange(2 * HALF + 1)[:, None, None]).astype(jnp.float32)
    toeplitz = jnp.einsum("bt,trm->brm", profile.astype(jnp.float32), choose)
    return toeplitz.reshape(4 * strip_rows, strip_rows + 2 * HALF).astype(jnp.bfloat16)


def body(template, science, variance, bad_pixels, intersection_patch, intersection_block):
    profile = basis_taps()
    visit_count, block_count, strip_rows, block_width = science.shape
    device_count = lax.axis_size("visit")
    own_index = lax.axis_index("visit")
    slot_count = visit_count * block_count
    capacity = max(2, -(-slot_count // device_count))
    block_span = block_width + 2 * MARGIN
    padded_rows = strip_rows + 2 * HALF
    all_patch, all_block = (
        lax.all_gather(intersection_patch, "visit", axis=0, tiled=True),
        lax.all_gather(intersection_block, "visit", axis=0, tiled=True),
    )
    source_patch = all_patch.reshape(device_count, slot_count)
    source_block = all_block.reshape(device_count, slot_count)
    slot_index = jnp.arange(slot_count)
    earlier = slot_index[None, :] < slot_index[:, None]
    same_patch = source_patch[:, :, None] == source_patch[:, None, :]
    source_rank = jnp.sum(same_patch & earlier[None], axis=2)
    own_patch = intersection_patch.reshape(slot_count)
    own_rank = lax.dynamic_index_in_dim(source_rank, own_index, 0, keepdims=False)
    own_slot = own_patch * capacity + own_rank
    wanted = (source_patch == own_index)[:, None, :] & (
        source_rank[:, None, :] == jnp.arange(capacity)[None, :, None]
    )
    at_block = source_block[:, :, None] == jnp.arange(NBLK)[None, None, :]
    chooser = jnp.einsum(
        "uck,uko->uco", wanted.astype(jnp.float32), at_block.astype(jnp.float32)
    ).astype(jnp.bfloat16)
    rimmed_strip = extended(template[0], (("template", 0),), HALF)
    strips = lax.all_gather(rimmed_strip[None], "visit", axis=0, tiled=True)
    own_block = intersection_block.reshape(slot_count)

    def cut_block(patch_id, column_block):
        return lax.dynamic_slice(
            strips, (patch_id, 0, column_block * block_width), (1, padded_rows, block_span)
        )[0]

    gathered_blocks = jax.vmap(cut_block)(own_patch, own_block)
    gathered_blocks = gathered_blocks.reshape(visit_count, block_count, padded_rows, block_span)
    across = column_table(profile, block_span, block_width)
    vertical = row_table(profile, strip_rows)
    usable = (1 - bad_pixels).astype(jnp.bfloat16)

    def convolve(inputs):
        blocks, signal, usable_mask = inputs
        smooth = jnp.einsum(
            "jmn,nx->jmx", blocks, across, preferred_element_type=jnp.float32
        ).astype(jnp.bfloat16)
        images = jnp.einsum(
            "ym,jmx->jyx", vertical, smooth, preferred_element_type=jnp.float32
        ).astype(jnp.bfloat16)
        basis_images = images.reshape(block_count, 4, strip_rows, 4, block_width)
        weighted = basis_images * usable_mask[:, None, :, None, :]
        cross_terms = jnp.einsum(
            "jbrac,jdrec->bade", weighted, basis_images, preferred_element_type=jnp.float32
        ).reshape(16, 16)
        with_ones = jnp.einsum(
            "jbrac,jrc->ba", basis_images, usable_mask, preferred_element_type=jnp.float32
        ).reshape(16)
        masked_signal = signal * usable_mask
        with_signal = jnp.einsum(
            "jbrac,jrc->ba", basis_images, masked_signal, preferred_element_type=jnp.float32
        ).reshape(16)
        usable_total = jnp.sum(usable_mask.astype(jnp.float32))
        signal_total = jnp.sum(masked_signal.astype(jnp.float32))
        upper_rows = jnp.concatenate(
            [cross_terms, with_ones[:, None], with_signal[:, None]], axis=1
        )
        bottom = jnp.concatenate([with_ones, usable_total[None], signal_total[None]])[None]
        return (images, jnp.concatenate([upper_rows, bottom], axis=0))

    images_all, partial_sums = lax.map(convolve, (gathered_blocks, science, usable))
    normal = lax.psum(partial_sums, "template")
    ridge_term = RIDGE * (normal[:, 16, 16] + 1.0)
    system = normal + ridge_term[:, None, None] * jnp.eye(17, 18, dtype=jnp.float32)[None]
    fitted = solve_normal(jnp.transpose(system, (1, 2, 0)))

    def differ(inputs):
        images, signal, noise_var, usable_mask, fit_row = inputs
        basis_images = images.reshape(block_count, 4, strip_rows, 4, block_width).astype(
            jnp.float32
        )
        modeled = (
            jnp.einsum(
                "jbrac,ba->jrc",
                basis_images,
                fit_row[:16].reshape(4, 4),
                precision=lax.Precision.HIGHEST,
            )
            + fit_row[16]
        )
        difference = signal.astype(jnp.float32) - modeled
        weight = usable_mask.astype(jnp.float32) / noise_var.astype(jnp.float32)
        return jnp.stack(
            [(weight * difference).astype(jnp.bfloat16), weight.astype(jnp.bfloat16)], axis=1
        )

    payload = lax.map(differ, (images_all, science, variance, usable, fitted.T))
    payload = payload.reshape(slot_count, 2 * strip_rows * block_width)
    placement = (own_slot[None, :] == jnp.arange(device_count * capacity)[:, None]).astype(
        jnp.bfloat16
    )
    outgoing = jnp.einsum(
        "sk,kx->sx", placement, payload, preferred_element_type=jnp.float32
    ).astype(jnp.bfloat16)
    outgoing = outgoing.reshape(device_count, capacity, 2, strip_rows, block_width)
    incoming = lax.all_to_all(outgoing, "visit", split_axis=0, concat_axis=0, tiled=True)
    accumulated = jnp.einsum(
        "uco,ucqrx->oqrx", chooser, incoming, preferred_element_type=jnp.float32
    )
    significance = accumulated[:, 0] / jnp.sqrt(jnp.maximum(accumulated[:, 1], 1.0))
    return significance.transpose(1, 0, 2).reshape(1, strip_rows, NBLK * block_width)


def solution(mesh):
    return jax.shard_map(
        body,
        mesh=mesh,
        in_specs=(
            P("visit", "template", None),
            P("visit", None, "template", None),
            P("visit", None, "template", None),
            P("visit", None, "template", None),
            P("visit", None),
            P("visit", None),
        ),
        out_specs=P("visit", "template", None),
        check_vma=False,
    )
```

profile of v0, /device:TPU:6, one launch (start us, length us, event | category | flops | bytes accessed | tf_op | source)
XLA Modules:
  0.0 547.4 jit_solution(14429271509945404964)
XLA Ops:
  6.5 0.8 slice_bitcast_fusion.1
  7.4 1.9 collective-permute-start
  9.3 3.6 collective-permute-start.1
  13.0 1.6 collective-permute-done.1
  14.6 1.6 maximum_bitcast_fusion.3
  19.4 106.7 %all-gather.1 = s32[64,6,4]{1,2,0:T(4,128)S(1)} all-gather(s32[1,6,4]{1,2,0:T(4,128)} %bitcast.457), channel_id=1, replica_groups=mesh['visit'=64,'template'=8] {'visit'}, dimensions={0}, use_global_device_ids=true | all-gather | bytes 6240 | tf_op jit(solution)/shard_map/all_gather | solution.py:76
  127.7 49.8 %all-gather.6.cloned.1.call-done = bf16[64,52,1152]{2,1,0:T(8,128)(2,1)} async-done(((bf16[1,52,1152]{2,1,0:T(8,128)(2,1)}), bf16[64,52,1152]{2,1,0:T(8,128)(2,1)}) %all-gather.6.cloned.1.call-update) | async-done | bytes 7667728 | tf_op jit(solution)/shard_map/all_gather | solution.py:96
  177.5 29.8 %copy.313 = bf16[64,52,1152]{1,0,2:T(8,128)(2,1)} copy(bf16[64,52,1152]{2,1,0:T(8,128)(2,1)} %all-gather.6.cloned.1.call-done) | data formatting | bytes 15335424 | tf_op jit(solution)/shard_map/all_gather | solution.py:96
  207.2 8.5 %gather_fusion = bf16[24,52,256]{1,0,2:T(8,128)(2,1)S(1)} fusion(bf16[64,52,1152]{1,0,2:T(8,128)(2,1)} %copy.313, s32[24]{0:T(128)S(1)} %fusion.71), kind=kCustom, calls=%fused_computation | custom fusion | bytes 1278240 | tf_op jit(solution)/shard_map/vmap()/gather | solution.py:100
  215.8 1.2 copy.315
  217.0 49.1 %while.22 = (s32[]{:T(128)}, bf16[6,4,128,512]{2,3,1,0:T(8,128)(2,1)}, f32[6,17,18]{2,0,1:T(8,128)S(1)}, bf16[6,4,52,256]{3,2,1,0:T(8,128)(2,1)S(1)}, bf16[256,5...) while((s32[]{:T(128)}, ...), condition=%wide.region_5.6_spmd, body=%wide.region_2.5_spmd.sunk | while | flops 91956152 | bytes 9150269 | solution.py:138
  217.0 1.4 bitcast_dynamic-update-slice_fusion.2
  218.8 2.4 fusion.105
  222.0 1.4 maximum_bitcast_fusion.6
  225.3 1.3 bitcast_dynamic-update-slice_fusion.2
  227.0 2.4 fusion.105
  230.2 1.4 maximum_bitcast_fusion.6
  233.4 1.3 bitcast_dynamic-update-slice_fusion.2
  235.1 2.4 fusion.105
  238.3 1.4 maximum_bitcast_fusion.6
  241.6 1.3 bitcast_dynamic-update-slice_fusion.2
  243.3 2.4 fusion.105
  246.5 1.4 maximum_bitcast_fusion.6
  249.7 1.4 bitcast_dynamic-update-slice_fusion.2
  251.5 2.4 fusion.105
  254.7 1.4 maximum_bitcast_fusion.6
  257.9 1.4 bitcast_dynamic-update-slice_fusion.2
  259.7 2.4 fusion.105
  262.9 1.4 maximum_bitcast_fusion.6
  266.1 21.6 %psum.7 = f32[6,17,18]{2,0,1:T(8,128)S(1)} all-reduce(f32[6,17,18]{2,0,1:T(8,128)S(1)} %get-tuple-element.86), channel_id=1, replica_groups=mesh['visit'=64,'template'=8] {'template'}, use_global_device_ids=true, to_apply=%region_6.7 | all-reduce | flops 1836 | bytes 14688 | tf_op jit(solution)/shard_map/psum | solution.py:139
  304.5 30.3 %while.23 = (s32[]{:T(128)}, bf16[6,4,2,32,128]{4,3,2,1,0:T(8,128)(2,1)S(1)}, bf16[6,4,32,128]{3,2,1,0:T(8,128)(2,1)S(1)}, bf16[6,4,32,128]{3,2,1,0:T(8,128)(2,1...) while((s32[]{:T(128)}, ...), condition=%wide.region_8.9_spmd, body=%wide.region_7.8_spmd.sunk | while | flops 3473410 | bytes 4162109 | solution.py:164
  304.6 1.1 constant_dynamic-slice_fusion.4
  307.3 1.4 fusion.109
  309.7 1.1 constant_dynamic-slice_fusion.4
  312.3 1.4 fusion.109
  313.7 0.8 convert_bitcast_fusion.2
  314.7 1.1 constant_dynamic-slice_fusion.4
  317.3 1.4 fusion.109
  319.7 1.1 constant_dynamic-slice_fusion.4
  322.3 1.4 fusion.109
  324.7 1.1 constant_dynamic-slice_fusion.4
  327.3 1.4 fusion.109
  329.7 1.1 constant_dynamic-slice_fusion.4
  332.4 1.4 fusion.109
  336.3 5.2 copy.354
  341.6 9.5 %all-to-all-start = ((bf16[64,2,2,32,128]{4,1,3,2,0:T(2,128)(2,1)}), bf16[64,2,2,32,128]{4,1,3,2,0:T(2,128)(2,1)S(1)}, u32[]{:S(2)}, u32[]{:S(2)}) async-start(bf16[64,2,2,32,128]{4,1,3,2,0:T(2,128)(2,1)} %copy.354), calls=%async_computation | async-start | bytes 4194304 | tf_op jit(solution)/shard_map/all_to_all | solution.py:173
  351.3 185.8 %all-gather.2 = s32[64,6,4]{1,2,0:T(4,128)S(1)} all-gather(s32[1,6,4]{1,2,0:T(4,128)S(1)} %bitcast.458), channel_id=1, replica_groups=mesh['visit'=64,'template'=8] {'visit'}, dimensions={0}, use_global_device_ids=true | all-gather | bytes 6240 | tf_op jit(solution)/shard_map/all_gather | solution.py:77
  537.5 2.3 fusion.26
  (300 shorter events, 55.7 us)
Async XLA Ops:
  6.5 121.1 %copy-start.1 = (s32[6,4,32,128]{3,2,1,0:T(8,128)S(1)}, s32[6,4,32,128]{3,2,1,0:T(8,128)}, u32[]{:S(2)}) copy-start(s32[6,4,32,128]{3,2,1,0:T(8,128)} %param.13) | copy-start | bytes 1179652
  6.5 170.9 %all-gather.6.cloned.1.call-start = ((), (), s32[]{:S(2)}) async-start(), calls=%async_computation.1 | async-start | bytes 8386560 | tf_op jit(solution)/shard_map/all_gather | solution.py:96
  7.4 5.6 %collective-permute-start = (bf16[10,1152]{1,0:T(8,128)(2,1)S(1)}, bf16[10,1152]{1,0:T(8,128)(2,1)S(1)}, u32[]{:S(2)}, u32[]{:S(2)}) collective-permute-start(bf16[10,1152]{1,0:T(8,128)(2,1)S(1)} %get-tuple-element.214), channel_id=1, source_target_pairs={{0,1},{1,2},{2,3},{3,4},{4,5},{5,6},{6,7},{8,9},{9,10},{10,11},{11... | collective-permute-start | bytes 69128 | tf_op jit(solution)/shard_map/ppermute | solution.py:19
  9.3 5.3 collective-permute-start.1
  207.2 9.8 %copy-start = (bf16[6,4,32,128]{3,2,1,0:T(8,128)(2,1)S(1)}, bf16[6,4,32,128]{3,2,1,0:T(8,128)(2,1)}, u32[]{:S(2)}) copy-start(bf16[6,4,32,128]{3,2,1,0:T(8,128)(2,1)} %param.11) | copy-start | bytes 589828
  341.6 9.7 %copy-start.2 = (s32[6,4]{0,1:T(4,128)S(1)}, s32[6,4]{0,1:T(4,128)}, u32[]{:S(2)}) copy-start(s32[6,4]{0,1:T(4,128)} %param.15) | copy-start | bytes 292
  341.6 196.0 %all-to-all-start = ((bf16[64,2,2,32,128]{4,1,3,2,0:T(2,128)(2,1)}), bf16[64,2,2,32,128]{4,1,3,2,0:T(2,128)(2,1)S(1)}, u32[]{:S(2)}, u32[]{:S(2)}) async-start(bf16[64,2,2,32,128]{4,1,3,2,0:T(2,128)(2,1)} %copy.354), calls=%async_computation | async-start | bytes 4194304 | tf_op jit(solution)/shard_map/all_to_all | solution.py:173
Sparse Core Ops, SparseCore 0:
  16.3 161.1 all-gather.5
where the time goes:
time: 549 us; the launch traced here: 547 us
  blocking collectives  314 us (57%)
  local copies, waits for them, and re-layouts  75.3 us (14%)
  waiting for transfers between devices  51.4 us (9%)
  other arithmetic  39.7 us (7%)
  matrix products  36.9 us (7%)
  starting transfers between devices  15.1 us (3%)
  between operations  13.9 us (3%)
    all_gather x1, blocking collectives, body(): lax.all_gather(intersection_block, 'visit', axis=0, tiled=True)  186 us
    all_gather x1, blocking collectives, body(): lax.all_gather(intersection_patch, 'visit', axis=0, tiled=True)  107 us
    all_gather x1, waiting for transfers between devices, body(): strips = lax.all_gather(rimmed_strip[None], 'visit', axis=0, tiled=True)  49.8 us
    all_gather x1, local copies, waits for them, and re-layouts, body(): strips = lax.all_gather(rimmed_strip[None], 'visit', axis=0, tiled=True)  29.8 us
    psum x1, blocking collectives, body(): normal = lax.psum(partial_sums, 'template')  21.6 us
    dot_general x6, matrix products, convolve(): jnp.einsum('jbrac,jrc->ba', basis_images, usable_mask, preferred_element_...  14.3 us
  transfers between devices with their start and end apart: 4, of which 2 were waited for; matrix products, arithmetic and copies ran while one was open for 1% of the time, Pallas kernels for 0%

commit v1 on v0

--- a/solution.py
+++ b/solution.py
@@ -73,7 +73,10 @@
     block_span = block_width + 2 * MARGIN
     padded_rows = strip_rows + 2 * HALF
     all_patch, all_block = (
-        lax.all_gather(intersection_patch, "visit", axis=0, tiled=True),
+        jnp.concatenate(
+            lax.all_to_all(jnp.stack([intersection_patch] * lax.axis_size("visit")), "visit", 0, 0),
+            axis=0,
+        ),
         lax.all_gather(intersection_block, "visit", axis=0, tiled=True),
     )
     source_patch = all_patch.reshape(device_count, slot_count)

time: 549 us -> 550 us (level)
  blocking collectives: 314 us -> 208 us
  waiting for transfers between devices: 51.4 us -> 137 us
  starting transfers between devices: 15.1 us -> 33.8 us
    all_gather x1 -> x0, blocking collectives: 107 us -> none  [body(): lax.all_gather(intersection_patch, 'visit', axis=0, tiled=True)]
    all_gather x1, waiting for transfers between devices: 49.8 us -> 125 us  [body(): strips = lax.all_gather(rimmed_strip[None], 'visit', axis=0, tiled=True)]
    all_to_all x0 -> x1, starting transfers between devices: none -> 18.7 us  [body(): lax.all_to_all(jnp.stack([intersection_patch] * lax.axis_size('visit')),...]
    all_to_all x0 -> x1, waiting for transfers between devices: none -> 11 us  [body(): lax.all_to_all(jnp.stack([intersection_patch] * lax.axis_size('visit')),...]
  transfers between devices with their start and end apart: 4 -> 5, of which waited for: 2 -> 3; matrix products, arithmetic and copies ran while one was open for 1% -> 1% of each run, Pallas kernels for 0% -> 0%
where the time goes in v1:
time: 550 us; the launch traced here: 548 us
  blocking collectives  208 us (38%)
  waiting for transfers between devices  137 us (25%)
  local copies, waits for them, and re-layouts  76.6 us (14%)
  other arithmetic  40.6 us (7%)
  matrix products  36.9 us (7%)
  starting transfers between devices  33.8 us (6%)
  between operations  13.9 us (3%)
    all_gather x1, blocking collectives, body(): lax.all_gather(intersection_block, 'visit', axis=0, tiled=True)  186 us
    all_gather x1, waiting for transfers between devices, body(): strips = lax.all_gather(rimmed_strip[None], 'visit', axis=0, tiled=True)  125 us
    all_gather x1, local copies, waits for them, and re-layouts, body(): strips = lax.all_gather(rimmed_strip[None], 'visit', axis=0, tiled=True)  29.8 us
    psum x1, blocking collectives, body(): normal = lax.psum(partial_sums, 'template')  21.5 us
    all_to_all x1, starting transfers between devices, body(): lax.all_to_all(jnp.stack([intersection_patch] * lax.axis_size('visit')),...  18.7 us
    dot_general x6, matrix products, convolve(): jnp.einsum('jbrac,jrc->ba', basis_images, usable_mask, preferred_element_...  14.3 us
  transfers between devices with their start and end apart: 5, of which 3 were waited for; matrix products, arithmetic and copies ran while one was open for 1% of the time, Pallas kernels for 0%

profile of v1, /device:TPU:6, one launch (start us, length us, event | category | flops | bytes accessed | tf_op | source)
XLA Modules:
  0.0 547.9 jit_solution(9077385758904027652)
XLA Ops:
  7.3 1.9 collective-permute-start
  9.3 3.6 collective-permute-start.1
  12.9 1.6 collective-permute-done.1
  14.5 1.6 maximum_bitcast_fusion.3
  16.1 1.4 stack.8
  17.5 18.7 %all-to-all-start = ((s32[64,6,4]{1,2,0:T(4,128)}), s32[64,6,4]{1,2,0:T(4,128)S(1)}, u32[]{:S(2)}, u32[]{:S(2)}) async-start(s32[64,6,4]{1,2,0:T(4,128)} %stack.8), calls=%async_computation | async-start | bytes 262144 | tf_op jit(solution)/shard_map/all_to_all | solution.py:77
  41.5 11.0 %all-to-all-done = s32[64,6,4]{1,2,0:T(4,128)S(1)} async-done(((s32[64,6,4]{1,2,0:T(4,128)}), s32[64,6,4]{1,2,0:T(4,128)S(1)}, u32[]{:S(2)}, u32[]{:S(2)}) %all-to-all-start) | async-done | bytes 6176 | tf_op jit(solution)/shard_map/all_to_all | solution.py:77
  53.0 124.8 %all-gather.5.cloned.1.call-done = bf16[64,52,1152]{2,1,0:T(8,128)(2,1)} async-done(((bf16[1,52,1152]{2,1,0:T(8,128)(2,1)}), bf16[64,52,1152]{2,1,0:T(8,128)(2,1)}) %all-gather.5.cloned.1.call-update) | async-done | bytes 7667728 | tf_op jit(solution)/shard_map/all_gather | solution.py:99
  177.8 29.8 %copy.376 = bf16[64,52,1152]{1,0,2:T(8,128)(2,1)} copy(bf16[64,52,1152]{2,1,0:T(8,128)(2,1)} %all-gather.5.cloned.1.call-done) | data formatting | bytes 15335424 | tf_op jit(solution)/shard_map/all_gather | solution.py:99
  207.6 8.5 %gather_fusion = bf16[24,52,256]{1,0,2:T(8,128)(2,1)S(1)} fusion(bf16[64,52,1152]{1,0,2:T(8,128)(2,1)} %copy.376, s32[24]{0:T(128)S(1)} %fusion.71), kind=kCustom, calls=%fused_computation | custom fusion | bytes 1278240 | tf_op jit(solution)/shard_map/vmap()/gather | solution.py:103
  216.1 1.2 copy.378
  217.4 49.1 %while.22 = (s32[]{:T(128)}, bf16[6,4,128,512]{2,3,1,0:T(8,128)(2,1)}, f32[6,17,18]{2,0,1:T(8,128)S(1)}, bf16[6,4,52,256]{3,2,1,0:T(8,128)(2,1)S(1)}, bf16[256,5...) while((s32[]{:T(128)}, ...), condition=%wide.region_5.6_spmd, body=%wide.region_2.5_spmd.sunk | while | flops 91956152 | bytes 9150269 | solution.py:141
  217.4 1.4 bitcast_dynamic-update-slice_fusion.2
  219.1 2.4 fusion.105
  222.3 1.4 maximum_bitcast_fusion.6
  225.6 1.3 bitcast_dynamic-update-slice_fusion.2
  227.3 2.4 fusion.105
  230.5 1.4 maximum_bitcast_fusion.6
  233.8 1.3 bitcast_dynamic-update-slice_fusion.2
  235.5 2.4 fusion.105
  238.7 1.4 maximum_bitcast_fusion.6
  241.9 1.3 bitcast_dynamic-update-slice_fusion.2
  243.6 2.4 fusion.105
  246.8 1.4 maximum_bitcast_fusion.6
  250.1 1.4 bitcast_dynamic-update-slice_fusion.2
  251.8 2.4 fusion.105
  255.0 1.4 maximum_bitcast_fusion.6
  258.3 1.4 bitcast_dynamic-update-slice_fusion.2
  260.1 2.4 fusion.105
  263.3 1.4 maximum_bitcast_fusion.6
  266.5 21.5 %psum.7 = f32[6,17,18]{2,0,1:T(8,128)S(1)} all-reduce(f32[6,17,18]{2,0,1:T(8,128)S(1)} %get-tuple-element.86), channel_id=1, replica_groups=mesh['visit'=64,'template'=8] {'template'}, use_global_device_ids=true, to_apply=%region_6.7 | all-reduce | flops 1836 | bytes 14688 | tf_op jit(solution)/shard_map/psum | solution.py:142
  304.8 30.3 %while.23 = (s32[]{:T(128)}, bf16[6,4,2,32,128]{4,3,2,1,0:T(8,128)(2,1)S(1)}, bf16[6,4,32,128]{3,2,1,0:T(8,128)(2,1)S(1)}, bf16[6,4,32,128]{3,2,1,0:T(8,128)(2,1...) while((s32[]{:T(128)}, ...), condition=%wide.region_8.9_spmd, body=%wide.region_7.8_spmd.sunk | while | flops 3473410 | bytes 4162109 | solution.py:167
  305.0 1.1 constant_dynamic-slice_fusion.4
  307.6 1.4 fusion.109
  310.0 1.1 constant_dynamic-slice_fusion.4
  312.6 1.4 fusion.109
  315.0 1.1 constant_dynamic-slice_fusion.4
  317.6 1.4 fusion.109
  320.0 1.1 constant_dynamic-slice_fusion.4
  322.7 1.4 fusion.109
  325.0 1.1 constant_dynamic-slice_fusion.4
  327.7 1.4 fusion.109
  330.1 1.1 constant_dynamic-slice_fusion.4
  332.7 1.4 fusion.109
  336.6 5.2 copy.417
  341.9 9.5 %all-to-all-start.1 = ((bf16[64,2,2,32,128]{4,1,3,2,0:T(2,128)(2,1)}), bf16[64,2,2,32,128]{4,1,3,2,0:T(2,128)(2,1)S(1)}, u32[]{:S(2)}, u32[]{:S(2)}) async-start(bf16[64,2,2,32,128]{4,1,3,2,0:T(2,128)(2,1)} %copy.417), calls=%async_computation.1 | async-start | bytes 4194304 | tf_op jit(solution)/shard_map/all_to_all | solution.py:176
  351.4 186.0 %all-gather.1 = s32[64,6,4]{1,2,0:T(4,128)S(1)} all-gather(s32[1,6,4]{1,2,0:T(4,128)S(1)} %bitcast.456), channel_id=1, replica_groups=mesh['visit'=64,'template'=8] {'visit'}, dimensions={0}, use_global_device_ids=true | all-gather | bytes 6240 | tf_op jit(solution)/shard_map/all_gather | solution.py:80
  538.1 2.3 fusion.26
  (300 shorter events, 58.2 us)
Async XLA Ops:
  6.5 171.2 %all-gather.5.cloned.1.call-start = ((), (), s32[]{:S(2)}) async-start(), calls=%async_computation.2 | async-start | bytes 8386560 | tf_op jit(solution)/shard_map/all_gather | solution.py:99
  7.3 5.6 %collective-permute-start = (bf16[10,1152]{1,0:T(8,128)(2,1)S(1)}, bf16[10,1152]{1,0:T(8,128)(2,1)S(1)}, u32[]{:S(2)}, u32[]{:S(2)}) collective-permute-start(bf16[10,1152]{1,0:T(8,128)(2,1)S(1)} %get-tuple-element.229), channel_id=1, source_target_pairs={{0,1},{1,2},{2,3},{3,4},{4,5},{5,6},{6,7},{8,9},{9,10},{10,11},{11... | collective-permute-start | bytes 69128 | tf_op jit(solution)/shard_map/ppermute | solution.py:19
  9.3 5.3 collective-permute-start.1
  17.5 35.0 %all-to-all-start = ((s32[64,6,4]{1,2,0:T(4,128)}), s32[64,6,4]{1,2,0:T(4,128)S(1)}, u32[]{:S(2)}, u32[]{:S(2)}) async-start(s32[64,6,4]{1,2,0:T(4,128)} %stack.8), calls=%async_computation | async-start | bytes 262144 | tf_op jit(solution)/shard_map/all_to_all | solution.py:77
  207.6 9.8 %copy-start = (bf16[6,4,32,128]{3,2,1,0:T(8,128)(2,1)S(1)}, bf16[6,4,32,128]{3,2,1,0:T(8,128)(2,1)}, u32[]{:S(2)}) copy-start(bf16[6,4,32,128]{3,2,1,0:T(8,128)(2,1)} %param.11) | copy-start | bytes 589828
  341.9 9.5 %copy-start.1 = (s32[6,4]{0,1:T(4,128)S(1)}, s32[6,4]{0,1:T(4,128)}, u32[]{:S(2)}) copy-start(s32[6,4]{0,1:T(4,128)} %param.15) | copy-start | bytes 292
  341.9 196.2 %all-to-all-start.1 = ((bf16[64,2,2,32,128]{4,1,3,2,0:T(2,128)(2,1)}), bf16[64,2,2,32,128]{4,1,3,2,0:T(2,128)(2,1)S(1)}, u32[]{:S(2)}, u32[]{:S(2)}) async-start(bf16[64,2,2,32,128]{4,1,3,2,0:T(2,128)(2,1)} %copy.417), calls=%async_computation.1 | async-start | bytes 4194304 | tf_op jit(solution)/shard_map/all_to_all | solution.py:176
Sparse Core Ops, SparseCore 0:
  16.2 161.4 all-gather.4
